TPU v7x, 32 devices: a whole 2x2x4 slice. The times are simulated.
32 devices in a mesh: tm: 8 (over z, x), state: 4 (over y, core).
Axes of the slice: x: 2, y: 2, z: 4, core: 2. Of those that a mesh axis runs over, the one named last changes fastest.
Arguments:
- trans_weight: bfloat16 [8, 2048, 2048], P('tm', None, 'state'), may hold values from 6e-06 to 163000
- pattern: int32 [16, 16], replicated, may hold values 0 or 1
- boundary: int32 [8], P('tm'), may hold values 0 or 1
- log_emit: float32 [8, 2048], P('tm', 'state'), may hold values from -63 to 153
Outputs:
- quad_op: float32 [4096, 2048], P('tm', 'state')
All inputs are finite; a program needn't handle non-finite values. No bound on the sum of `boundary` on one device may be relied on, other than what follows from the above.
Results may differ from a plain program's by a relative error of at most 0.0003.
Values sent between devices are 32-bit elements; how exact they have to be, the bound alone decides.
A program may use at most 64 MiB of HBM per device.

v0:
```python
import jax
import jax.numpy as jnp
from jax import lax
from jax.sharding import PartitionSpec as P

BLOCK = 128


def from_partner(shard, axis, apart):
    return lax.ppermute(shard, axis, [(i, i ^ 1 << apart) for i in range(lax.axis_size(axis))])


def block_mask(pattern, row_count, col_start, col_count):
    block_count = pattern.shape[0]
    row_ids = jnp.arange(row_count, dtype=jnp.int32) // BLOCK
    col_ids = (col_start + jnp.arange(col_count, dtype=jnp.int32)) // BLOCK
    blocks = jnp.arange(block_count, dtype=jnp.int32)
    row_hot = (row_ids[:, None] == blocks[None, :]).astype(jnp.float32)
    col_hot = (blocks[:, None] == col_ids[None, :]).astype(jnp.float32)
    lookup = pattern.astype(jnp.float32)
    return jnp.dot(jnp.dot(row_hot, lookup), col_hot)


def combine(left_log, right_log):
    row_top = jnp.max(left_log, axis=1, keepdims=True)
    col_top = jnp.max(right_log, axis=0, keepdims=True)
    lead = jnp.exp(left_log - row_top).astype(jnp.bfloat16)
    trail = jnp.exp(right_log - col_top).astype(jnp.bfloat16)
    summed = jnp.dot(lead, trail, preferred_element_type=jnp.float32)
    return row_top + col_top + jnp.log(summed)


def on_device(trans_weight, pattern, boundary, log_emit):
    weight = trans_weight[0]
    states, col_width = weight.shape
    col_start = lax.axis_index("state") * col_width
    restart = 0.0001 + 0.4999 * boundary.astype(jnp.float32)
    mask_table = block_mask(pattern, states, col_start, col_width)
    mixture = (1.0 - restart) * (4.0 / states) * weight.astype(
        jnp.float32
    ) * mask_table + restart / states
    own_op = jnp.log(mixture) + log_emit
    tm_index = lax.axis_index("tm")
    half_index = tm_index % 2
    partner_op = from_partner(own_op, "tm", 0)
    first_op = jnp.where(half_index == 0, own_op, partner_op)
    second_op = jnp.where(half_index == 0, partner_op, own_op)
    row_start = half_index * (states // 2)
    row_count = states // 2
    left_slab = lax.dynamic_slice_in_dim(first_op, row_start, row_count, 0)
    left_full = lax.all_gather(left_slab, "state", axis=1, tiled=True)
    pair_op = combine(left_full, second_op)
    other_half = from_partner(pair_op, "tm", 0)
    own_pair = jnp.where(
        half_index == 0,
        jnp.concatenate([pair_op, other_half], axis=0),
        jnp.concatenate([other_half, pair_op], axis=0),
    )
    other_pair = from_partner(own_pair, "tm", 1)
    leading = tm_index // 2 % 2 == 0
    quarter = states // 4
    quarter_start = tm_index % 4 * quarter
    own_rows = lax.dynamic_slice_in_dim(own_pair, quarter_start, quarter, 0)
    other_rows = lax.dynamic_slice_in_dim(other_pair, quarter_start, quarter, 0)
    quad_slab = jnp.where(leading, own_rows, other_rows)
    right_pair = jnp.where(leading, other_pair, own_pair)
    quad_left = lax.all_gather(quad_slab, "state", axis=1, tiled=True)
    return combine(quad_left, right_pair)


def solution(mesh):
    return jax.shard_map(
        on_device,
        mesh=mesh,
        in_specs=(P("tm", None, "state"), P(), P("tm"), P("tm", "state")),
        out_specs=P("tm", "state"),
        check_vma=False,
    )
```

profile of v0, /device:TPU:25, one launch (start us, length us, event | category | flops | bytes accessed | tf_op | source)
XLA Modules:
  0.0 374.4 jit_solution(6337932703887638775)
XLA Ops:
  6.5 0.0 all-gather.3.cloned.1.call-start
  7.2 5.0 %fusion.3 = f32[2048,512]{1,0:T(8,128)} fusion(bf16[1,2048,512]{2,1,0:T(8,128)(2,1)} %param.4, f32[512]{0:T(512)} %bitcast.11, f32[]{:T(128)} %bitcast.2, f32[]{:T(128)} %bitcast, s32[2048]{0:T(1024)S(1)} %add_select_fusion, s32[512]{0:T(512)S(1)} %add_select_fusion.1, s32[16,16]{1,0:T(8,128)} %param.5), kind=kOutput, calls=%fused_computation.6 | convolution fusion | flops 39887104 | bytes 6304776 | tf_op jit(solution)/shard_map/dot_general | solution.py:21
  12.2 1.2 collective-permute-start
  13.4 90.5 %collective-permute-done = f32[2048,512]{1,0:T(8,128)} collective-permute-done((f32[2048,512]{1,0:T(8,128)}, f32[2048,512]{1,0:T(8,128)}, u32[]{:S(2)}, u32[]{:S(2)}) %collective-permute-start) | collective-permute-done | bytes 4194336 | tf_op jit(solution)/shard_map/ppermute | solution.py:10
  103.9 4.0 %dynamic-slice_select_fusion = f32[1024,512]{1,0:T(8,128)} fusion(f32[2048,512]{1,0:T(8,128)} %collective-permute-done, s32[]{:T(128)S(6)} %select_n.82, f32[2048,512]{1,0:T(8,128)} %fusion.3, pred[]{:T(512)S(6)} %eq.39), kind=kLoop, calls=%fused_computation.12 | loop fusion | flops 524288 | bytes 6291461 | tf_op jit(solution)/shard_map/jit(_where)/select_n | solution.py:46
  108.0 0.0 all-gather.3.cloned.1.call-update
  108.0 0.0 all-gather.5.cloned.1.call-start
  108.1 2.7 fusion.9
  110.8 58.0 %all-gather.3.cloned.1.call-done = f32[1024,2048]{1,0:T(8,128)} async-done(((f32[1024,512]{1,0:T(8,128)}), f32[1024,2048]{1,0:T(8,128)}) %all-gather.3.cloned.1.call-update) | async-done | bytes 8388624 | tf_op jit(solution)/shard_map/all_gather | solution.py:51
  168.7 3.8 %reduce_max.36 = f32[1024]{0:T(1024)S(1)} reduce(f32[1024,2048]{1,0:T(8,128)} %all-gather.3.cloned.1.call-done, f32[]{:T(128)} %constant.88.clone.1), dimensions={1}, to_apply=%region_0.1 | reduce | flops 2096128 | bytes 8392708 | tf_op jit(solution)/shard_map/reduce_max | solution.py:25
  172.6 6.5 %log_add_fusion = f32[1024,512]{1,0:T(8,128)S(1)} fusion(f32[512]{0:T(512)S(1)} %fusion.9, f32[2048,512]{1,0:T(8,128)} %collective-permute-done, f32[2048,512]{1,0:T(8,128)} %fusion.3, pred[]{:T(512)S(6)} %eq.39, f32[1024,2048]{1,0:T(8,128)} %all-gather.3.cloned.1.call-done, f32[1024]{0:T(1024)S(1)} %reduce_max.36), kind=kOutput, calls=%fused_computation.15 | convolution fusion | flops 2155872256 | bytes 18880512 | tf_op jit(solution)/shard_map/dot_general | solution.py:29
  179.1 1.3 collective-permute-start.1
  180.3 45.8 %collective-permute-done.1 = f32[1024,512]{1,0:T(8,128)S(1)} collective-permute-done((f32[1024,512]{1,0:T(8,128)S(1)}, f32[1024,512]{1,0:T(8,128)S(1)}, u32[]{:S(2)}, u32[]{:S(2)}) %collective-permute-start.1) | collective-permute-done | bytes 2097184 | tf_op jit(solution)/shard_map/ppermute | solution.py:10
  226.1 2.8 maximum_select_fusion
  228.9 0.3 collective-permute-start.2
  229.2 91.1 %collective-permute-done.2 = f32[2048,512]{1,0:T(8,128)} collective-permute-done((f32[2048,512]{1,0:T(8,128)}, f32[2048,512]{1,0:T(8,128)}, u32[]{:S(2)}, u32[]{:S(2)}) %collective-permute-start.2) | collective-permute-done | bytes 4194336 | tf_op jit(solution)/shard_map/ppermute | solution.py:10
  320.2 2.7 dynamic-slice_select_fusion.1
  323.0 0.0 all-gather.5.cloned.1.call-update
  323.0 2.7 fusion.10
  325.7 33.6 %all-gather.5.cloned.1.call-done = f32[512,2048]{1,0:T(8,128)} async-done(((f32[512,512]{1,0:T(8,128)}), f32[512,2048]{1,0:T(8,128)}) %all-gather.5.cloned.1.call-update) | async-done | bytes 4194320 | tf_op jit(solution)/shard_map/all_gather | solution.py:67
  359.3 2.5 reduce_max.38
  361.8 5.8 %add_add_fusion = f32[512,512]{1,0:T(8,128)} fusion(f32[512]{0:T(512)S(1)} %fusion.10, f32[512]{0:T(512)S(1)} %reduce_max.38, f32[2048,512]{1,0:T(8,128)} %collective-permute-done.2, f32[2048,512]{1,0:T(8,128)} %maximum_select_fusion, pred[]{:T(512)S(6)} %eq.38, f32[512,2048]{1,0:T(8,128)} %all-gather.5.cloned.1.call-done), kind=kOutput, calls=%fused_computation.23 | convolution fusion | flops 1079508992 | bytes 13635585 | tf_op jit(solution)/shard_map/dot_general | solution.py:29
  (2 shorter events, 0.0 us)
Async XLA Ops:
  6.5 162.2 %all-gather.3.cloned.1.call-start = ((), (), s32[]{:S(2)}) async-start(), calls=%async_computation | async-start | bytes 10485760 | tf_op jit(solution)/shard_map/all_gather | solution.py:51
  12.2 91.8 %collective-permute-start = (f32[2048,512]{1,0:T(8,128)}, f32[2048,512]{1,0:T(8,128)}, u32[]{:S(2)}, u32[]{:S(2)}) collective-permute-start(f32[2048,512]{1,0:T(8,128)} %fusion.3), channel_id=1, source_target_pairs={{0,4},{4,0},{8,12},{12,8},{16,20},{20,16},{24,28},{28,24},{1,5},{5... | collective-permute-start | bytes 12582920 | tf_op jit(solution)/shard_map/ppermute | solution.py:10
  108.0 251.3 %all-gather.5.cloned.1.call-start = ((), (), s32[]{:S(2)}) async-start(), calls=%async_computation.1 | async-start | bytes 5242880 | tf_op jit(solution)/shard_map/all_gather | solution.py:67
  179.1 47.0 %collective-permute-start.1 = (f32[1024,512]{1,0:T(8,128)S(1)}, f32[1024,512]{1,0:T(8,128)S(1)}, u32[]{:S(2)}, u32[]{:S(2)}) collective-permute-start(f32[1024,512]{1,0:T(8,128)S(1)} %log_add_fusion), channel_id=1, source_target_pairs={{0,4},{4,0},{8,12},{12,8},{16,20},{20,16},{24,28},{28,24},{1,5},{5... | collective-permute-start | bytes 6291464 | tf_op jit(solution)/shard_map/ppermute | solution.py:10
  228.9 91.3 %collective-permute-start.2 = (f32[2048,512]{1,0:T(8,128)}, f32[2048,512]{1,0:T(8,128)}, u32[]{:S(2)}, u32[]{:S(2)}) collective-permute-start(f32[2048,512]{1,0:T(8,128)} %maximum_select_fusion), channel_id=1, source_target_pairs={{0,8},{4,12},{8,0},{12,4},{16,24},{20,28},{24,16},{28,20},{1,9},{5... | collective-permute-start | bytes 12582920 | tf_op jit(solution)/shard_map/ppermute | solution.py:10
Sparse Core Ops, SparseCore 0:
  108.1 60.5 all-gather.2
  323.1 36.1 all-gather.4
where the time goes:
time: 376 us; the launch traced here: 374 us
  waiting for transfers between devices  319 us (85%)
  other arithmetic  21.3 us (6%)
  matrix products  17.2 us (5%)
  between operations  14.1 us (4%)
    ppermute x3, waiting for transfers between devices, from_partner(): lax.ppermute(shard, axis, [(i, i ^ 1 << apart) for i in range(lax.axis_si...  227 us
    all_gather x1, waiting for transfers between devices, on_device(): left_full = lax.all_gather(left_slab, 'state', axis=1, tiled=True)  58 us
    all_gather x1, waiting for transfers between devices, on_device(): quad_left = lax.all_gather(quad_slab, 'state', axis=1, tiled=True)  33.6 us
    dot_general x2, matrix products, combine(): summed = jnp.dot(lead, trail, preferred_element_type=jnp.float32)  12.3 us
  transfers between devices with their start and end apart: 5, of which 5 were waited for; matrix products, arithmetic and copies ran while one was open for 1% of the time, Pallas kernels for 0%

commit v1 on v0

v1 whole, which is shorter than its diff:
```python
import functools
import math

import jax
import jax.numpy as jnp
from jax import lax
from jax.experimental import pallas as pl
from jax.experimental.pallas import tpu as pltpu
from jax.sharding import PartitionSpec as P

BLOCK = 128
ROWS = 64
LEAD_SHIFT = 12
TRAIL_SHIFT = -49
MESH = pl.DeviceIdType.MESH


def kernel(
    parts, w_ref, aux_ref, out_ref, left, trail, pair, first, stage, infos,
    info_send, info_recv, x_send, x_recv, y_send, y_recv, p_send, p_recv,
    q_send, q_recv, g_send, g_recv,
):
    states, width = w_ref.shape
    blocks = states // BLOCK
    chunks = states // ROWS
    per_quarter = chunks // 4
    tm = lax.axis_index("tm")
    s = lax.axis_index("state")
    base = tm // 4 * 4
    member = tm % 4
    p = member // 2
    h = member % 2
    me = member * parts + s
    core = s + 1 - 2 * (s % 2)
    over = (s + 2) % 4
    far = (core + 2) % 4
    total = 4 * parts

    def device(p_, h_, s_):
        return (base + 2 * p_ + h_, s_)

    barrier = pltpu.get_barrier_semaphore()
    for k in range(1, total):
        peer = (me + k) % total
        pl.semaphore_signal(barrier, inc=1, device_id=(base + peer // parts, peer % parts), device_id_type=MESH)
    pl.semaphore_wait(barrier, total - 1)

    info = aux_ref.at[pl.ds(blocks, 8)]

    def info_copy(k):
        peer = (me + k) % total
        return pltpu.make_async_remote_copy(
            src_ref=info, dst_ref=infos.at[me], send_sem=info_send.at[k], recv_sem=info_recv.at[k],
            device_id=(base + peer // parts, peer % parts), device_id_type=MESH)

    for k in range(1, total):
        info_copy(k).start()
    infos[me] = aux_ref[blocks:blocks + 8, :]

    def rows_of(i):
        quarter = (i + 2) % 4
        return pl.multiple_of((quarter * per_quarter + i // 4) * ROWS, ROWS)

    def remote(ref, slot, row, send, recv, target):
        view = ref.at[slot, pl.ds(row, ROWS)] if slot is not None else ref.at[pl.ds(row, ROWS)]
        return pltpu.make_async_remote_copy(
            src_ref=view, dst_ref=view, send_sem=send, recv_sem=recv, device_id=target, device_id_type=MESH)

    def x_copy(i):
        return remote(left, s, rows_of(i), x_send.at[i], x_recv.at[i], device(p, 1 - h, s))

    def y_copy(kind, i, slot, target):
        return remote(left, slot, rows_of(i), y_send.at[kind, i], y_recv.at[kind, i], device(p, h, target))

    def pair_copy(kind, i, target):
        return remote(pair, None, rows_of(i), p_send.at[kind, i], p_recv.at[i], target)

    def g_copy(kind, g, slot, target):
        row = pl.multiple_of(g * ROWS, ROWS)
        return remote(first, slot, row, g_send.at[kind, g], g_recv.at[kind, g], device(p, h, target))

    def q_copy(i):
        quarter = (i + 2) % 4
        g = i // 4
        return pltpu.make_async_remote_copy(
            src_ref=stage.at[pl.ds(rows_of(i), ROWS)],
            dst_ref=first.at[s, pl.ds(pl.multiple_of(g * ROWS, ROWS), ROWS)],
            send_sem=q_send.at[i], recv_sem=q_recv.at[g],
            device_id=(base + quarter, s), device_id_type=MESH)

    def odds(row):
        gain = aux_ref[pl.ds(row // BLOCK, 1), :]
        return 1.0 + w_ref[pl.ds(row, ROWS), :].astype(jnp.float32) * gain

    @pl.when(h == 0)
    def _():
        def send_chunk(i, c):
            row = rows_of(i)
            left[s, pl.ds(row, ROWS), :] = odds(row)
            x_copy(i).start()
            return c
        lax.fori_loop(0, chunks, send_chunk, 0)

    @pl.when(h == 1)
    def _():
        def make_trail(i, c):
            row = rows_of(i)
            trail[pl.ds(row, ROWS), :] = odds(row).astype(jnp.bfloat16)
            return c
        lax.fori_loop(0, chunks, make_trail, 0)

    def wait_info(k):
        sender = (me + total - k) % total
        pltpu.make_async_remote_copy(
            src_ref=info, dst_ref=infos.at[sender], send_sem=info_send.at[k], recv_sem=info_recv.at[k],
            device_id=(base + sender // parts, sender % parts), device_id_type=MESH).wait_recv()

    for k in range(1, total):
        wait_info(k)
        info_copy(k).wait_send()

    def emission(m, part):
        return infos[m * parts + part, 0:1, :]

    def peak(m):
        top = emission(m, 0)
        for part in range(1, parts):
            top = jnp.maximum(top, emission(m, part))
        return jnp.max(top, axis=1, keepdims=True)

    left_peak = jnp.where(p == 0, peak(0), peak(2))
    weights = [
        jnp.exp(jnp.where(p == 0, emission(0, part), emission(2, part)) - left_peak) for part in range(parts)
    ]
    middle_peak = peak(1)
    own_emission = aux_ref[blocks:blocks + 1, :]
    col_scale = jnp.where(
        p == 0, jnp.exp(own_emission - middle_peak) * 2.0 ** LEAD_SHIFT, jnp.full_like(own_emission, 2.0 ** TRAIL_SHIFT)
    )

    def combine(i):
        row = rows_of(i)
        acc = None
        for part in range(parts):
            lead = (left[part, pl.ds(row, ROWS), :] * weights[part]).astype(jnp.bfloat16)
            term = jnp.dot(lead, trail[part * width:(part + 1) * width, :], preferred_element_type=jnp.float32)
            acc = term if acc is None else acc + term
        return acc * col_scale

    def step(t, c):
        @pl.when(h == 1)
        def _():
            @pl.when(t < chunks)
            def _():
                x_copy(t).wait_recv()
                y_copy(0, t, s, core).start()
                y_copy(1, t, s, over).start()

            @pl.when((t >= 1) & (t < chunks + 1))
            def _():
                i = t - 1
                y_copy(1, i, over, over).wait_recv()
                y_copy(2, i, over, core).start()

            @pl.when((t >= 2) & (t < chunks + 2))
            def _():
                i = t - 2
                y_copy(0, i, core, core).wait_recv()
                y_copy(2, i, far, core).wait_recv()
                value = combine(i)
                row = rows_of(i)

                @pl.when(p == 1)
                def _():
                    pair[pl.ds(row, ROWS), :] = value
                    pair_copy(0, i, device(0, 1, s)).start()
                    pair_copy(1, i, device(1, 0, s)).start()

                @pl.when((p == 0) & ((i + 2) % 4 == 1))
                def _():
                    first[s, pl.ds(pl.multiple_of(i // 4 * ROWS, ROWS), ROWS), :] = value

                @pl.when((p == 0) & ((i + 2) % 4 != 1))
                def _():
                    stage[pl.ds(row, ROWS), :] = value
                    q_copy(i).start()

        @pl.when((h == 0) & (p == 1) & (t >= 3) & (t < chunks + 3))
        def _():
            i = t - 3
            pair_copy(0, i, device(0, 0, s)).wait_recv()
            pair_copy(0, i, device(0, 0, s)).start()

        @pl.when((t >= 7) & ((t - 7) % 4 == 0) & ((t - 7) // 4 < per_quarter))
        def _():
            g = (t - 7) // 4

            @pl.when(member != 1)
            def _():
                pltpu.make_async_remote_copy(
                    src_ref=stage.at[pl.ds(0, ROWS)],
                    dst_ref=first.at[s, pl.ds(pl.multiple_of(g * ROWS, ROWS), ROWS)],
                    send_sem=q_send.at[g], recv_sem=q_recv.at[g],
                    device_id=device(0, 1, over), device_id_type=MESH).wait_recv()
            g_copy(0, g, s, core).start()
            g_copy(1, g, s, over).start()

        @pl.when((t >= 9) & ((t - 9) % 4 == 0))
        def _():
            g = (t - 9) // 4
            g_copy(1, g, over, over).wait_recv()
            g_copy(2, g, over, core).start()
        return c

    lax.fori_loop(0, chunks + 6, step, 0)

    @pl.when(p == 0)
    def _():
        def wait_pair(i, c):
            pair_copy(0, i, device(1, h, s)).wait_recv()
            return c
        lax.fori_loop(0, chunks, wait_pair, 0)

    def to_trail(i, c):
        row = pl.multiple_of(i * ROWS, ROWS)
        trail[pl.ds(row, ROWS), :] = pair[pl.ds(row, ROWS), :].astype(jnp.bfloat16)
        return c

    lax.fori_loop(0, chunks, to_trail, 0)

    def wait_gather(g, c):
        g_copy(0, g, core, core).wait_recv()
        g_copy(2, g, far, core).wait_recv()
        return c

    lax.fori_loop(0, per_quarter, wait_gather, 0)

    log_shares = infos[0, 1:2, :] + infos[parts, 1:2, :] + infos[2 * parts, 1:2, :] + infos[3 * parts, 1:2, :]
    shift = math.log(2.0) * (LEAD_SHIFT + TRAIL_SHIFT)
    last_emission = jnp.zeros_like(own_emission)
    for part in range(parts):
        last_emission = jnp.where(s == part, emission(3, part), last_emission)
    offset = last_emission + log_shares + (peak(0) + middle_peak + peak(2) - shift)

    out_rows = out_ref.shape[0]
    tile = 128

    def finish(i, c):
        row = pl.multiple_of(i * tile, tile)
        acc = None
        for part in range(parts):
            term = jnp.dot(
                first[part, pl.ds(row, tile), :].astype(jnp.bfloat16), trail[part * width:(part + 1) * width, :],
                preferred_element_type=jnp.float32)
            acc = term if acc is None else acc + term
        out_ref[pl.ds(row, tile), :] = jnp.log(acc) + offset
        return c

    lax.fori_loop(0, out_rows // tile, finish, 0)

    @pl.when(h == 0)
    def _():
        def drain(i, c):
            x_copy(i).wait_send()
            return c
        lax.fori_loop(0, chunks, drain, 0)

        @pl.when(p == 1)
        def _():
            def drain_pair(i, c):
                pair_copy(0, i, device(0, 0, s)).wait_send()
                return c
            lax.fori_loop(0, chunks, drain_pair, 0)

    @pl.when(h == 1)
    def _():
        def drain(i, c):
            y_copy(0, i, s, core).wait_send()
            y_copy(1, i, s, over).wait_send()
            y_copy(2, i, over, core).wait_send()

            @pl.when(p == 1)
            def _():
                pair_copy(0, i, device(0, 1, s)).wait_send()
                pair_copy(1, i, device(1, 0, s)).wait_send()

            @pl.when((p == 0) & ((i + 2) % 4 != 1))
            def _():
                q_copy(i).wait_send()
            return c
        lax.fori_loop(0, chunks, drain, 0)

    def drain_gather(g, c):
        g_copy(0, g, s, core).wait_send()
        g_copy(1, g, s, over).wait_send()
        g_copy(2, g, over, core).wait_send()
        return c

    lax.fori_loop(0, per_quarter, drain_gather, 0)


def on_device(parts, trans_weight, pattern, boundary, log_emit):
    weight = trans_weight[0]
    states, width = weight.shape
    blocks = pattern.shape[0]
    restart = 0.0001 + 0.4999 * boundary.astype(jnp.float32)
    first_block = lax.axis_index("state") * (width // BLOCK)
    mine = lax.dynamic_slice_in_dim(pattern, first_block, width // BLOCK, 1).astype(jnp.float32)
    gain = jnp.repeat(mine, BLOCK, axis=1) * (4.0 * (1.0 - restart) / restart)
    share = jnp.broadcast_to(jnp.log(restart / states)[:, None], (7, width))
    aux = jnp.concatenate([gain, log_emit, share], axis=0)
    chunks = states // ROWS
    dma = pltpu.SemaphoreType.DMA
    vmem = pl.BlockSpec(memory_space=pltpu.VMEM)
    return pl.pallas_call(
        functools.partial(kernel, parts),
        out_shape=jax.ShapeDtypeStruct((states // 4, width), jnp.float32),
        in_specs=[vmem, vmem],
        out_specs=vmem,
        scratch_shapes=[
            pltpu.VMEM((parts, states, width), jnp.float32),
            pltpu.VMEM((states, width), jnp.bfloat16),
            pltpu.VMEM((states, width), jnp.float32),
            pltpu.VMEM((parts, states // 4, width), jnp.float32),
            pltpu.VMEM((states, width), jnp.float32),
            pltpu.VMEM((4 * parts, 8, width), jnp.float32),
            dma((4 * parts,)), dma((4 * parts,)),
            dma((chunks,)), dma((chunks,)),
            dma((3, chunks)), dma((3, chunks)),
            dma((2, chunks)), dma((chunks,)),
            dma((chunks,)), dma((chunks // 4,)),
            dma((3, chunks // 4)), dma((3, chunks // 4)),
        ],
        compiler_params=pltpu.CompilerParams(
            collective_id=0, has_side_effects=True, vmem_limit_bytes=52 * 1024 * 1024
        ),
    )(weight, aux)


def solution(mesh):
    return jax.shard_map(
        functools.partial(on_device, mesh.shape["state"]),
        mesh=mesh,
        in_specs=(P("tm", None, "state"), P(), P("tm"), P("tm", "state")),
        out_specs=P("tm", "state"),
        check_vma=False,
    )
```

time: 376 us -> 149 us (0.40)
  waiting for transfers between devices: 319 us -> 0 us
  Pallas kernels: 0 us -> 144 us
  other arithmetic: 21.3 us -> 1.53 us
  matrix products: 17.2 us -> 0 us
  between operations: 14.1 us -> 0.76 us
    ppermute x3 -> x0, waiting for transfers between devices: 227 us -> none  [from_partner(): lax.ppermute(shard, axis, [(i, i ^ 1 << apart) for i in range(lax.axis_si...]
    pallas_call x0 -> x1, Pallas kernels: none -> 144 us  [on_device(): pl.pallas_call(functools.partial(kernel, parts), out_shape=jax.ShapeDtype...]
    all_gather x2 -> x0, waiting for transfers between devices: 91.6 us -> none  [the longest x1 58 us: on_device(): left_full = lax.all_gather(left_slab, 'state', axis=1, tiled=True)]
    dot_general x3 -> x0, matrix products: 17.2 us -> none  [the longest x2 12.3 us: combine(): summed = jnp.dot(lead, trail, preferred_element_type=jnp.float32)]
    reduce_max x4 -> x0, other arithmetic: 11.7 us -> none  [the longest x2 6.28 us: combine(): row_top = jnp.max(left_log, axis=1, keepdims=True)]
    select_n x5 -> x0, other arithmetic: 9.6 us -> none  [the longest x1 4.05 us: on_device(): first_op = jnp.where(half_index == 0, own_op, partner_op)]
  transfers between devices with their start and end apart: 5 -> 0, of which waited for: 5 -> 0; matrix products, arithmetic and copies ran while one was open for 1% -> 0% of each run, Pallas kernels for 0% -> 0%
where the time goes in v1:
time: 149 us; the launch traced here: 148 us
  Pallas kernels  144 us (97%)
  other arithmetic  1.53 us (1%)
    pallas_call x1, Pallas kernels, on_device(): pl.pallas_call(functools.partial(kernel, parts), out_shape=jax.ShapeDtype...  144 us

profile of v1, /device:TPU:25, one launch (start us, length us, event | category | flops | bytes accessed | tf_op | source)
XLA Modules:
  0.0 147.9 jit_solution(9040548100622431535)
XLA Ops:
  0.7 0.1 pad.2.clone
  0.8 0.8 convert_multiply_fusion
  1.6 0.1 broadcast_in_dim.12
  1.7 0.8 maximum_maximum_fusion.aux_ref
  2.4 144.4 %shard_map.46 = f32[512,512]{1,0:T(8,128)S(1)} custom-call(bf16[2048,512]{1,0:T(8,128)(2,1)} %bitcast.7, f32[24,512]{1,0:T(8,128)S(1)} %maximum_maximum_fusion.aux_ref), custom_call_target="tpu_custom_call" | custom-call | tf_op jit(solution)/shard_map/pallas_call | solution.py:315
  146.9 1.0 copy.10
  (2 shorter events, 0.0 us)

commit v2 on v1

v2 whole, which is shorter than its diff:
```python
import functools
import math

import jax
import jax.numpy as jnp
from jax import lax
from jax.experimental import pallas as pl
from jax.experimental.pallas import tpu as pltpu
from jax.sharding import PartitionSpec as P

BLOCK = 128
ROWS = 64
STRIPS = 4
TILE = 256
SCHEDULE = (
    (0, 16, 0, None), (16, 19, None, 0), (19, 21, 1, None), (21, 24, None, 1), (24, 26, 2, None), (26, 30, None, 2),
    (30, 32, 3, 3),
)
LEAD_SHIFT = 12
TRAIL_SHIFT = -49
MESH = pl.DeviceIdType.MESH


def kernel(
    parts, w_ref, aux_ref, out_ref, left, trail, pair, first, stage, right, infos,
    info_send, info_recv, x_send, x_recv, y_send, y_recv, p_send, p_recv,
    q_send, q_recv, g_send, g_recv, b_send, b_recv, w_send, w_recv, v_send, v_recv,
):
    states, width = w_ref.shape
    blocks = states // BLOCK
    chunks = states // ROWS
    per_quarter = chunks // 4
    half = chunks // 2
    quarter_rows = states // 4
    strip = width // STRIPS
    tm = lax.axis_index("tm")
    s = lax.axis_index("state")
    base = tm // 4 * 4
    member = tm % 4
    p = member // 2
    h = member % 2
    me = member * parts + s
    core = s + 1 - 2 * (s % 2)
    over = (s + 2) % 4
    far = (core + 2) % 4
    total = 4 * parts

    def device(p_, h_, s_):
        return (base + 2 * p_ + h_, s_)

    barrier = pltpu.get_barrier_semaphore()
    for k in range(1, total):
        peer = (me + k) % total
        pl.semaphore_signal(barrier, inc=1, device_id=(base + peer // parts, peer % parts), device_id_type=MESH)
    pl.semaphore_wait(barrier, total - 1)

    info = aux_ref.at[pl.ds(blocks, 8)]

    def info_copy(k):
        peer = (me + k) % total
        return pltpu.make_async_remote_copy(
            src_ref=info, dst_ref=infos.at[me], send_sem=info_send.at[k], recv_sem=info_recv.at[k],
            device_id=(base + peer // parts, peer % parts), device_id_type=MESH)

    for k in range(1, total):
        info_copy(k).start()
    infos[me] = aux_ref[blocks:blocks + 8, :]

    def rows_of(i):
        return pl.multiple_of(i * ROWS, ROWS)

    def remote(ref, slot, row, send, recv, target):
        view = ref.at[slot, pl.ds(row, ROWS)] if slot is not None else ref.at[pl.ds(row, ROWS)]
        return pltpu.make_async_remote_copy(
            src_ref=view, dst_ref=view, send_sem=send, recv_sem=recv, device_id=target, device_id_type=MESH)

    def half_rows(i, side):
        return pl.multiple_of(((2 + side - 2 * (i % 2)) * per_quarter + i // 2) * ROWS, ROWS)

    def x_copy(i, row):
        return remote(left, s, row, x_send.at[i], x_recv.at[i], device(p, 1 - h, s))

    def y_copy(kind, i, row, slot, target):
        return remote(left, slot, row, y_send.at[kind, i], y_recv.at[kind, i], device(p, h, target))

    def pair_copy(kind, i, target):
        return remote(pair, None, rows_of(i), p_send.at[kind, i], p_recv.at[i], target)

    def local_row(g):
        return pl.multiple_of(g * ROWS, ROWS)

    def g_copy(kind, g, slot, target):
        return remote(first, slot, local_row(g), g_send.at[kind, g], g_recv.at[kind, g], device(p, h, target))

    def columns(n):
        return pl.ds(n * strip, strip)

    def g_strip(kind, n, slot, target):
        view = first.at[slot, :, columns(n)]
        return pltpu.make_async_remote_copy(
            src_ref=view, dst_ref=view, send_sem=g_send.at[kind, n], recv_sem=g_recv.at[kind, n],
            device_id=device(p, h, target), device_id_type=MESH)

    def q_copy(g):
        return pltpu.make_async_remote_copy(
            src_ref=stage.at[pl.ds(local_row(g), ROWS)], dst_ref=first.at[s, pl.ds(local_row(g), ROWS)],
            send_sem=q_send.at[g], recv_sem=q_recv.at[g], device_id=device(1 - p, 1, s), device_id_type=MESH)

    def q_strip(n):
        return pltpu.make_async_remote_copy(
            src_ref=stage.at[pl.ds(0, quarter_rows), columns(n)], dst_ref=first.at[s, :, columns(n)],
            send_sem=q_send.at[n], recv_sem=q_recv.at[n], device_id=device(1 - p, 0, s), device_id_type=MESH)

    def w_copy(g):
        return pltpu.make_async_remote_copy(
            src_ref=stage.at[pl.ds(local_row(g), ROWS)], dst_ref=stage.at[pl.ds(local_row(g + per_quarter), ROWS)],
            send_sem=w_send.at[g], recv_sem=w_recv.at[g], device_id=device(p, h, over), device_id_type=MESH)

    def v_copy(g):
        return pltpu.make_async_remote_copy(
            src_ref=stage.at[pl.ds(local_row(g + per_quarter), ROWS)], dst_ref=first.at[over, pl.ds(local_row(g), ROWS)],
            send_sem=v_send.at[g], recv_sem=v_recv.at[g], device_id=device(1 - p, 1, s), device_id_type=MESH)

    def b_copy(n):
        view = right.at[:, columns(n)]
        return pltpu.make_async_remote_copy(
            src_ref=view, dst_ref=view, send_sem=b_send.at[n], recv_sem=b_recv.at[n],
            device_id=device(p, 1 - h, s), device_id_type=MESH)

    def odds(row):
        gain = aux_ref[pl.ds(row // BLOCK, 1), :]
        return 1.0 + w_ref[pl.ds(row, ROWS), :].astype(jnp.float32) * gain

    def loop(count, body):
        def run(i, c):
            body(i)
            return c
        lax.fori_loop(0, count, run, 0)

    @pl.when((h == 0) & (p == 1))
    def _():
        @functools.partial(loop, chunks)
        def _(i):
            row = rows_of(i)
            left[s, pl.ds(row, ROWS), :] = odds(row)
            x_copy(i, row).start()

    @pl.when((h == 0) & (p == 0))
    def _():
        @functools.partial(loop, half)
        def _(i):
            row = half_rows(i, 1)
            left[s, pl.ds(row, ROWS), :] = odds(row)
            x_copy(i, row).start()
            near = half_rows(i, 0)
            left[s, pl.ds(near, ROWS), :] = odds(near)
            y_copy(0, i, near, s, core).start()
            y_copy(1, i, near, s, over).start()

    @pl.when((h == 1) & (p == 1))
    def _():
        @functools.partial(loop, chunks)
        def _(i):
            row = local_row(i)
            trail[pl.ds(row, ROWS), :] = odds(row).astype(jnp.bfloat16)

    @pl.when((h == 1) & (p == 0))
    def _():
        for n in range(STRIPS):
            @functools.partial(loop, chunks)
            def _(i):
                row = local_row(i)
                gain = aux_ref[pl.ds(row // BLOCK, 1), :][:, n * strip:(n + 1) * strip]
                value = 1.0 + w_ref[pl.ds(row, ROWS), columns(n)].astype(jnp.float32) * gain
                right[pl.ds(row, ROWS), columns(n)] = value
                trail[pl.ds(row, ROWS), columns(n)] = value.astype(jnp.bfloat16)
            b_copy(n).start()

    def wait_info(k):
        sender = (me + total - k) % total
        pltpu.make_async_remote_copy(
            src_ref=info, dst_ref=infos.at[sender], send_sem=info_send.at[k], recv_sem=info_recv.at[k],
            device_id=(base + sender // parts, sender % parts), device_id_type=MESH).wait_recv()

    for k in range(1, total):
        wait_info(k)
        info_copy(k).wait_send()

    def emission(m, part):
        return infos[m * parts + part, 0:1, :]

    def peak(m):
        top = emission(m, 0)
        for part in range(1, parts):
            top = jnp.maximum(top, emission(m, part))
        return jnp.max(top, axis=1, keepdims=True)

    left_peak = jnp.where(p == 0, peak(0), peak(2))
    weights = [
        jnp.exp(jnp.where(p == 0, emission(0, part), emission(2, part)) - left_peak) for part in range(parts)
    ]
    middle_peak = peak(1)
    middle_emission = infos[parts + s, 0:1, :]
    middle_scale = jnp.exp(middle_emission - middle_peak) * 2.0 ** LEAD_SHIFT

    def product(row, count, n):
        acc = None
        for part in range(parts):
            lead = (left[part, pl.ds(row, count), :] * weights[part]).astype(jnp.bfloat16)
            block = slice(part * width, (part + 1) * width)
            right_block = trail[block, :] if n is None else trail[block, n * strip:(n + 1) * strip]
            term = jnp.dot(lead, right_block, preferred_element_type=jnp.float32)
            acc = term if acc is None else acc + term
        return acc

    def take(i, row):
        x_copy(i, row).wait_recv()
        y_copy(0, i, row, s, core).start()
        y_copy(1, i, row, s, over).start()

    def relay(i, row):
        y_copy(1, i, row, over, over).wait_recv()
        y_copy(2, i, row, over, core).start()

    def have(i, row):
        y_copy(0, i, row, core, core).wait_recv()
        y_copy(2, i, row, far, core).wait_recv()

    @pl.when((p == 1) & (h == 1))
    def _():
        @functools.partial(loop, chunks + 2)
        def _(t):
            @pl.when(t < chunks)
            def _():
                take(t, rows_of(t))

            @pl.when((t >= 1) & (t < chunks + 1))
            def _():
                relay(t - 1, rows_of(t - 1))

            @pl.when((t >= 3) & (t % 2 == 1))
            def _():
                i = t - 3
                row = pl.multiple_of(rows_of(i), 2 * ROWS)
                have(i, rows_of(i))
                have(i + 1, rows_of(i + 1))
                pair[pl.ds(row, 2 * ROWS), :] = product(row, 2 * ROWS, None) * 2.0 ** TRAIL_SHIFT
                pair_copy(1, i, device(1, 0, s)).start()
                pair_copy(0, i, device(0, 1, s)).start()
                pair_copy(1, i + 1, device(1, 0, s)).start()
                pair_copy(0, i + 1, device(0, 1, s)).start()

            @pl.when((t >= 11) & ((t - 11) % 2 == 0) & ((t - 11) // 2 < per_quarter))
            def _():
                g = (t - 11) // 2
                q_copy(g).wait_recv()
                g_copy(0, g, s, core).start()
                v_copy(g).wait_recv()
                g_copy(2, g, over, core).start()

    @pl.when((p == 0) & (h == 1))
    def _():
        @functools.partial(loop, half + 5)
        def _(t):
            @pl.when(t < half)
            def _():
                take(t, half_rows(t, 1))

            @pl.when((t >= 1) & (t < half + 1))
            def _():
                relay(t - 1, half_rows(t - 1, 1))

            @pl.when((t >= 2) & (t < half + 2))
            def _():
                i = t - 2
                g = i // 2
                row = half_rows(i, 1)
                have(i, row)
                value = product(row, ROWS, None) * middle_scale

                @pl.when(i % 2 == 0)
                def _():
                    stage[pl.ds(local_row(g), ROWS), :] = value
                    w_copy(g).start()
                    q_copy(g).start()

                @pl.when(i % 2 == 1)
                def _():
                    first[s, pl.ds(local_row(g), ROWS), :] = value
                    g_copy(1, g, s, over).start()
                    g_copy(0, g, s, core).start()

            @pl.when(t >= 5)
            def _():
                i = t - 5
                g = i // 2

                @pl.when(i % 2 == 0)
                def _():
                    w_copy(g).wait_recv()
                    v_copy(g).start()

                @pl.when(i % 2 == 1)
                def _():
                    g_copy(1, g, over, over).wait_recv()
                    g_copy(2, g, over, core).start()

    def strip_out(n):
        g_strip(1, n, s, over).start()
        g_strip(0, n, s, core).start()

    def strip_relay(n):
        g_strip(1, n, over, over).wait_recv()
        g_strip(2, n, over, core).start()

    @pl.when((p == 1) & (h == 0))
    def _():
        for low, high, arrive, pass_on in SCHEDULE:
            def relay_pair(i, c):
                pair_copy(0, i, device(0, 0, s)).wait_recv()
                pair_copy(0, i, device(0, 0, s)).start()
                return c
            lax.fori_loop(chunks * low // 32, chunks * high // 32, relay_pair, 0)
            if arrive is not None:
                q_strip(arrive).wait_recv()
                strip_out(arrive)
            if pass_on is not None:
                strip_relay(pass_on)

    @pl.when((p == 0) & (h == 0))
    def _():
        @functools.partial(loop, half)
        def _(i):
            relay(i, half_rows(i, 0))

        @functools.partial(loop, half)
        def _(i):
            have(i, half_rows(i, 0))

        for n in range(STRIPS):
            b_copy(n).wait_recv()

            @functools.partial(loop, chunks)
            def _(i):
                row = local_row(i)
                trail[pl.ds(row, ROWS), columns(n)] = right[pl.ds(row, ROWS), columns(n)].astype(jnp.bfloat16)

            scale = middle_scale[:, n * strip:(n + 1) * strip]

            @functools.partial(loop, quarter_rows // TILE)
            def _(j):
                row = pl.multiple_of(j * TILE, TILE)
                source = pl.multiple_of(2 * quarter_rows + j * TILE, TILE)
                stage[pl.ds(row, TILE), columns(n)] = product(source, TILE, n) * scale

            q_strip(n).start()

            @functools.partial(loop, quarter_rows // TILE)
            def _(j):
                row = pl.multiple_of(j * TILE, TILE)
                first[s, pl.ds(row, TILE), columns(n)] = product(row, TILE, n) * scale

            strip_out(n)
            if n > 0:
                strip_relay(n - 1)
        strip_relay(STRIPS - 1)

    @pl.when(p == 0)
    def _():
        @functools.partial(loop, chunks)
        def _(i):
            pair_copy(0, i, device(1, h, s)).wait_recv()

    def to_trail(i, c):
        row = pl.multiple_of(i * ROWS, ROWS)
        trail[pl.ds(row, ROWS), :] = pair[pl.ds(row, ROWS), :].astype(jnp.bfloat16)
        return c

    lax.fori_loop(0, chunks, to_trail, 0)

    @pl.when(h == 1)
    def _():
        @functools.partial(loop, per_quarter)
        def _(g):
            g_copy(0, g, core, core).wait_recv()
            g_copy(2, g, far, core).wait_recv()

    @pl.when(h == 0)
    def _():
        for n in range(STRIPS):
            g_strip(0, n, core, core).wait_recv()
            g_strip(2, n, far, core).wait_recv()

    log_shares = infos[0, 1:2, :] + infos[parts, 1:2, :] + infos[2 * parts, 1:2, :] + infos[3 * parts, 1:2, :]
    shift = math.log(2.0) * (LEAD_SHIFT + TRAIL_SHIFT)
    last_emission = jnp.zeros_like(middle_emission)
    for part in range(parts):
        last_emission = jnp.where(s == part, emission(3, part), last_emission)
    offset = last_emission + log_shares + (peak(0) + middle_peak + peak(2) - shift)

    out_rows = out_ref.shape[0]
    tile = 128

    def finish(i, c):
        row = pl.multiple_of(i * tile, tile)
        acc = None
        for part in range(parts):
            term = jnp.dot(
                first[part, pl.ds(row, tile), :].astype(jnp.bfloat16), trail[part * width:(part + 1) * width, :],
                preferred_element_type=jnp.float32)
            acc = term if acc is None else acc + term
        out_ref[pl.ds(row, tile), :] = jnp.log(acc) + offset
        return c

    lax.fori_loop(0, out_rows // tile, finish, 0)

    def drain_left(i, row):
        y_copy(0, i, row, s, core).wait_send()
        y_copy(1, i, row, s, over).wait_send()
        y_copy(2, i, row, over, core).wait_send()

    @pl.when((p == 1) & (h == 1))
    def _():
        @functools.partial(loop, chunks)
        def _(i):
            drain_left(i, rows_of(i))
            pair_copy(0, i, device(0, 1, s)).wait_send()
            pair_copy(1, i, device(1, 0, s)).wait_send()

        @functools.partial(loop, per_quarter)
        def _(g):
            g_copy(0, g, s, core).wait_send()
            g_copy(2, g, over, core).wait_send()

    @pl.when((p == 1) & (h == 0))
    def _():
        @functools.partial(loop, chunks)
        def _(i):
            x_copy(i, rows_of(i)).wait_send()
            pair_copy(0, i, device(0, 0, s)).wait_send()

    @pl.when((p == 0) & (h == 1))
    def _():
        for n in range(STRIPS):
            b_copy(n).wait_send()

        @functools.partial(loop, half)
        def _(i):
            drain_left(i, half_rows(i, 1))

        @functools.partial(loop, per_quarter)
        def _(g):
            q_copy(g).wait_send()
            w_copy(g).wait_send()
            v_copy(g).wait_send()
            g_copy(0, g, s, core).wait_send()
            g_copy(1, g, s, over).wait_send()
            g_copy(2, g, over, core).wait_send()

    @pl.when((p == 0) & (h == 0))
    def _():
        @functools.partial(loop, half)
        def _(i):
            x_copy(i, half_rows(i, 1)).wait_send()
            drain_left(i, half_rows(i, 0))

        for n in range(STRIPS):
            q_strip(n).wait_send()

    @pl.when(h == 0)
    def _():
        for n in range(STRIPS):
            g_strip(0, n, s, core).wait_send()
            g_strip(1, n, s, over).wait_send()
            g_strip(2, n, over, core).wait_send()


def on_device(parts, trans_weight, pattern, boundary, log_emit):
    weight = trans_weight[0]
    states, width = weight.shape
    blocks = pattern.shape[0]
    restart = 0.0001 + 0.4999 * boundary.astype(jnp.float32)
    first_block = lax.axis_index("state") * (width // BLOCK)
    mine = lax.dynamic_slice_in_dim(pattern, first_block, width // BLOCK, 1).astype(jnp.float32)
    gain = jnp.repeat(mine, BLOCK, axis=1) * (4.0 * (1.0 - restart) / restart)
    share = jnp.broadcast_to(jnp.log(restart / states)[:, None], (7, width))
    aux = jnp.concatenate([gain, log_emit, share], axis=0)
    chunks = states // ROWS
    dma = pltpu.SemaphoreType.DMA
    vmem = pl.BlockSpec(memory_space=pltpu.VMEM)
    return pl.pallas_call(
        functools.partial(kernel, parts),
        out_shape=jax.ShapeDtypeStruct((states // 4, width), jnp.float32),
        in_specs=[vmem, vmem],
        out_specs=vmem,
        scratch_shapes=[
            pltpu.VMEM((parts, states, width), jnp.float32),
            pltpu.VMEM((states, width), jnp.bfloat16),
            pltpu.VMEM((states, width), jnp.float32),
            pltpu.VMEM((parts, states // 4, width), jnp.float32),
            pltpu.VMEM((states, width), jnp.float32),
            pltpu.VMEM((states, width), jnp.float32),
            pltpu.VMEM((4 * parts, 8, width), jnp.float32),
            dma((4 * parts,)), dma((4 * parts,)),
            dma((chunks,)), dma((chunks,)),
            dma((3, chunks)), dma((3, chunks)),
            dma((2, chunks)), dma((chunks,)),
            dma((chunks // 4,)), dma((chunks // 4,)),
            dma((3, chunks // 4)), dma((3, chunks // 4)),
            dma((STRIPS,)), dma((STRIPS,)),
            dma((chunks // 4,)), dma((chunks // 4,)), dma((chunks // 4,)), dma((chunks // 4,)),
        ],
        compiler_params=pltpu.CompilerParams(
            collective_id=0, has_side_effects=True, vmem_limit_bytes=52 * 1024 * 1024
        ),
    )(weight, aux)


def solution(mesh):
    return jax.shard_map(
        functools.partial(on_device, mesh.shape["state"]),
        mesh=mesh,
        in_specs=(P("tm", None, "state"), P(), P("tm"), P("tm", "state")),
        out_specs=P("tm", "state"),
        check_vma=False,
    )
```

time: 149 us -> 157 us (1.054)
  Pallas kernels: 144 us -> 153 us
    pallas_call x1, Pallas kernels: 144 us -> 153 us  [on_device(): pl.pallas_call(functools.partial(kernel, parts), out_shape=jax.ShapeDtype...]
where the time goes in v2:
time: 157 us; the launch traced here: 156 us
  Pallas kernels  153 us (97%)
    pallas_call x1, Pallas kernels, on_device(): pl.pallas_call(functools.partial(kernel, parts), out_shape=jax.ShapeDtype...  153 us

profile of v2, /device:TPU:25, one launch (start us, length us, event | category | flops | bytes accessed | tf_op | source)
XLA Modules:
  0.0 156.4 jit_solution(3357715333796362845)
XLA Ops:
  0.7 0.1 pad.2.clone
  0.8 0.8 convert_multiply_fusion
  1.6 0.1 broadcast_in_dim.12
  1.7 0.8 maximum_maximum_fusion.aux_ref
  2.4 153.0 %shard_map.46 = f32[512,512]{1,0:T(8,128)S(1)} custom-call(bf16[2048,512]{1,0:T(8,128)(2,1)} %bitcast.7, f32[24,512]{1,0:T(8,128)S(1)} %maximum_maximum_fusion.aux_ref), custom_call_target="tpu_custom_call" | custom-call | tf_op jit(solution)/shard_map/pallas_call | solution.py:491
  155.5 1.0 copy.10
  (2 shorter events, 0.0 us)

commit v3 on v2

--- a/solution.py
+++ b/solution.py
@@ -250,13 +250,12 @@
                 pair_copy(1, i + 1, device(1, 0, s)).start()
                 pair_copy(0, i + 1, device(0, 1, s)).start()
 
-            @pl.when((t >= 11) & ((t - 11) % 2 == 0) & ((t - 11) // 2 < per_quarter))
-            def _():
-                g = (t - 11) // 2
-                q_copy(g).wait_recv()
-                g_copy(0, g, s, core).start()
-                v_copy(g).wait_recv()
-                g_copy(2, g, over, core).start()
+        @functools.partial(loop, per_quarter)
+        def _(g):
+            q_copy(g).wait_recv()
+            g_copy(0, g, s, core).start()
+            v_copy(g).wait_recv()
+            g_copy(2, g, over, core).start()
 
     @pl.when((p == 0) & (h == 1))
     def _():

time: 157 us -> 132 us (0.84)
  Pallas kernels: 153 us -> 128 us
    pallas_call x1, Pallas kernels: 153 us -> 128 us  [on_device(): pl.pallas_call(functools.partial(kernel, parts), out_shape=jax.ShapeDtype...]
where the time goes in v3:
time: 132 us
  Pallas kernels  128 us (97%)
  other arithmetic  1.53 us (1%)
    pallas_call x1, Pallas kernels, on_device(): pl.pallas_call(functools.partial(kernel, parts), out_shape=jax.ShapeDtype...  128 us

profile of v3, /device:TPU:25, one launch (start us, length us, event | category | flops | bytes accessed | tf_op | source)
XLA Modules:
  0.0 131.8 jit_solution(6843007830675083132)
XLA Ops:
  0.7 0.1 pad.2.clone
  0.8 0.8 convert_multiply_fusion
  1.6 0.1 broadcast_in_dim.12
  1.7 0.8 maximum_maximum_fusion.aux_ref
  2.4 128.4 %shard_map.46 = f32[512,512]{1,0:T(8,128)S(1)} custom-call(bf16[2048,512]{1,0:T(8,128)(2,1)} %bitcast.7, f32[24,512]{1,0:T(8,128)S(1)} %maximum_maximum_fusion.aux_ref), custom_call_target="tpu_custom_call" | custom-call | tf_op jit(solution)/shard_map/pallas_call | solution.py:490
  130.8 1.0 copy.10
  (2 shorter events, 0.0 us)

commit v4 on v3

--- a/solution.py
+++ b/solution.py
@@ -238,17 +238,14 @@
             def _():
                 relay(t - 1, rows_of(t - 1))
 
-            @pl.when((t >= 3) & (t % 2 == 1))
-            def _():
-                i = t - 3
-                row = pl.multiple_of(rows_of(i), 2 * ROWS)
-                have(i, rows_of(i))
-                have(i + 1, rows_of(i + 1))
-                pair[pl.ds(row, 2 * ROWS), :] = product(row, 2 * ROWS, None) * 2.0 ** TRAIL_SHIFT
+            @pl.when(t >= 2)
+            def _():
+                i = t - 2
+                row = rows_of(i)
+                have(i, row)
+                pair[pl.ds(row, ROWS), :] = product(row, ROWS, None) * 2.0 ** TRAIL_SHIFT
                 pair_copy(1, i, device(1, 0, s)).start()
                 pair_copy(0, i, device(0, 1, s)).start()
-                pair_copy(1, i + 1, device(1, 0, s)).start()
-                pair_copy(0, i + 1, device(0, 1, s)).start()
 
         @functools.partial(loop, per_quarter)
         def _(g):

time: 132 us -> 129 us (0.977)
  Pallas kernels: 128 us -> 125 us
    pallas_call x1, Pallas kernels: 128 us -> 125 us  [on_device(): pl.pallas_call(functools.partial(kernel, parts), out_shape=jax.ShapeDtype...]
where the time goes in v4:
time: 129 us
  Pallas kernels  125 us (97%)
  other arithmetic  1.53 us (1%)
    pallas_call x1, Pallas kernels, on_device(): pl.pallas_call(functools.partial(kernel, parts), out_shape=jax.ShapeDtype...  125 us

profile of v4, /device:TPU:25, one launch (start us, length us, event | category | flops | bytes accessed | tf_op | source)
XLA Modules:
  0.0 128.9 jit_solution(17374235239808025350)
XLA Ops:
  0.7 0.1 pad.2.clone
  0.8 0.8 convert_multiply_fusion
  1.6 0.1 broadcast_in_dim.12
  1.7 0.8 maximum_maximum_fusion.aux_ref
  2.4 125.5 %shard_map.46 = f32[512,512]{1,0:T(8,128)S(1)} custom-call(bf16[2048,512]{1,0:T(8,128)(2,1)} %bitcast.7, f32[24,512]{1,0:T(8,128)S(1)} %maximum_maximum_fusion.aux_ref), custom_call_target="tpu_custom_call" | custom-call | tf_op jit(solution)/shard_map/pallas_call | solution.py:487
  127.9 1.0 copy.10
  (2 shorter events, 0.0 us)
